TPU v7x, 32 devices: a whole 2x2x4 slice. The times are simulated.
32 devices in a mesh: seq: 8 (over z, core), chan: 4 (over y, x).
Axes of the slice: x: 2, y: 2, z: 4, core: 2. Of those that a mesh axis runs over, the one named last changes fastest.
Arguments:
- gate_raw: bfloat16 [8, 2048, 2048], P('seq', None, 'chan'), may hold values from -50 to 50
- value_raw: bfloat16 [8, 2048, 2048], P('seq', None, 'chan'), may hold values from -50 to 50
- filter_gate: float32 [7, 2048], P(None, 'chan'), may hold values from -3 to 3
- filter_value: float32 [7, 2048], P(None, 'chan'), may hold values from -3 to 3
- teacher: float32 [8, 2048, 2048], P('seq', 'chan'), may hold values from -0.25 to 1, as said below
Outputs:
- grad_gate_raw: bfloat16 [8, 2048, 2048], P('seq', None, 'chan')
- grad_value_raw: bfloat16 [8, 2048, 2048], P('seq', None, 'chan')
- grad_filter_gate: float32 [7, 2048], P(None, 'chan')
- grad_filter_value: float32 [7, 2048], P(None, 'chan')
Inputs may be any that keep to these rules, and one draw needn't show every extreme that they name: teacher[s] is symmetric for each of the 8 sequences, with ones on its diagonal.
All inputs are finite; a program needn't handle non-finite values.
Results may differ from a plain program's by a relative error of at most 0.0059.
Values may be sent and summed in bfloat16 or wider, within the bound.
A program may use at most 128 MiB of HBM per device.

v0:
```python
import functools
import math

import jax
import jax.numpy as jnp
from jax import lax
from jax.experimental import pallas as pl
from jax.experimental.pallas import tpu as pltpu
from jax.sharding import PartitionSpec as P

epsilon = 1e-06
PAD = 16
TILE = 64
MESH = pl.DeviceIdType.MESH


def kernel(
    groups, rings, taps, norm_factor,
    gate_in, value_in, filter_gate, filter_value, teacher_in,
    gate_out, value_out, gate_taps, value_taps,
    raw_g, raw_v, conv_g, conv_v, held, teach, own_n, block_n, total, outgoing, hgrad,
    sums, mine, others,
    in_sem, send_sem, recv_sem, a2a_send, a2a_recv, tap_send, tap_recv,
    near, teach_send_sem, teach_recv_sem,
):
    length, width = gate_in.shape[1:]
    stripe = length // groups
    full = width * groups
    factor = 16.0 / math.sqrt(length)
    tile = min(TILE, stripe)
    lanes = [slice(k, min(k + 128, width)) for k in range(0, width, 128)]
    f32, bf16 = jnp.float32, jnp.bfloat16
    me, ring = lax.axis_index("chan"), lax.axis_index("seq")
    paired = groups == 4 and rings % 2 == 0
    flip1 = lambda at: at + 1 - 2 * lax.rem(at, 2)
    flip2 = lambda at: lax.rem(at + 2, 4)
    flip3 = lambda at: 3 - at
    if paired:
        core = lax.rem(ring, 2)
        buddy = ring + 1 - 2 * core
        side = me // 2
        same = 1 - (core - side) * (core - side)
        base_at = same * me + (1 - same) * flip2(me)
        slot = same * me + (1 - same) * groups
        proc = ring - core + side
        is_home, is_guest = same == 1, same == 0
    else:
        base_at, slot, proc = me, me, ring

    def rows_of(chunk, size=stripe, start=0):
        return pl.ds(pl.multiple_of(chunk * stripe + start, math.gcd(stripe, start) if start else stripe), size)

    in_copies = []
    for c in range(groups):
        span = pl.ds(c * stripe, stripe)
        dest = pl.ds(PAD + c * stripe, stripe)
        for k, (src, dst) in enumerate(((gate_in, raw_g), (value_in, raw_v))):
            in_copies.append(pltpu.make_async_copy(src.at[0, span], dst.at[dest], in_sem.at[k, c]))
    for copy in in_copies:
        copy.start()
    teach_copy = pltpu.make_async_copy(teacher_in.at[0], teach, in_sem.at[2, 0])
    if paired:
        pl.when(is_home)(teach_copy.start)
    else:
        teach_copy.start()

    barrier = pltpu.get_barrier_semaphore()
    for step in range(1, groups):
        pl.semaphore_signal(barrier, inc=1, device_id=(ring, lax.rem(me + step, groups)), device_id_type=MESH)
        if paired:
            pl.semaphore_signal(barrier, inc=1, device_id=(buddy, lax.rem(me + step, groups)), device_id_type=MESH)
    greeted = (groups - 1) * (2 if paired else 1) + rings - 1
    for step in range(1, rings):
        pl.semaphore_signal(barrier, inc=1, device_id=(lax.rem(ring + step, rings), me), device_id_type=MESH)

    raw_g[0:PAD] = jnp.zeros((PAD, width), bf16)
    raw_v[0:PAD] = jnp.zeros((PAD, width), bf16)
    conv_g[length:] = jnp.zeros((PAD, width), f32)
    conv_v[length:] = jnp.zeros((PAD, width), f32)
    hgrad[length:] = jnp.zeros((PAD, width), bf16)
    sums[...] = jnp.zeros(sums.shape, f32)
    total[...] = jnp.zeros(total.shape, f32)
    for copy in in_copies:
        copy.wait()

    def conv_chunk(chunk):
        def body(i, _):
            base = pl.multiple_of(chunk * stripe + i * tile, tile)
            for lane in lanes:
                made = []
                for raw, weights, store in ((raw_g, filter_gate, conv_g), (raw_v, filter_value, conv_v)):
                    window = raw[pl.ds(base, tile + PAD), lane].astype(f32)
                    out = weights[0:1, lane] * window[PAD:]
                    for j in range(1, taps):
                        out = out + weights[j : j + 1, lane] * pltpu.roll(window, j, 0)[PAD:]
                    store[pl.ds(base, tile), lane] = out
                    made.append(out)
                held[slot, pl.ds(base, tile), lane] = (made[0] * made[1]).astype(bf16)
            return 0

        lax.fori_loop(0, stripe // tile, body, 0)

    def gather_copy(source, target, chunk, to, send):
        rows = rows_of(chunk)
        return pltpu.make_async_remote_copy(
            src_ref=held.at[source, rows], dst_ref=held.at[target, rows],
            send_sem=send, recv_sem=recv_sem.at[target, chunk],
            device_id=to, device_id_type=MESH,
        )

    def arrived(source, chunk):
        gather_copy(source, source, chunk, (ring, me), send_sem.at[0, 0]).wait_recv()

    if paired:
        far = pl.ds(pl.multiple_of(side * 2 * stripe, stripe), 2 * stripe)

        def teach_send(cols, dst, to, k):
            return pltpu.make_async_remote_copy(
                src_ref=teacher_in.at[0, :, cols], dst_ref=dst, send_sem=teach_send_sem.at[k],
                recv_sem=teach_recv_sem.at[k], device_id=to, device_id_type=MESH,
            )

        to_swap = teach_send(far, teach.at[:, far], (buddy, flip2(me)), 0)
        to_near = teach_send(rows_of(flip2(me)), near.at[0], (buddy, me), 1)
        to_next = teach_send(rows_of(flip3(me)), near.at[1], (buddy, flip1(me)), 2)
        far_in = pl.ds(pl.multiple_of((1 - side) * 2 * stripe, stripe), 2 * stripe)

        def to_x(chunk):
            return gather_copy(base_at, base_at, chunk, (ring, flip1(me)), send_sem.at[0, chunk])

        def to_buddy(chunk):
            return gather_copy(base_at, base_at, chunk, (buddy, me), send_sem.at[1, chunk])

        def pass_on(chunk):
            return gather_copy(flip1(base_at), flip1(base_at), chunk, (buddy, me), send_sem.at[2, chunk])

        def swap(chunk):
            return gather_copy(groups, me, chunk, (buddy, flip2(me)), send_sem.at[3, chunk])

        order = (flip1(me), flip3(me), me, flip2(me))
        pl.semaphore_wait(barrier, greeted)

        @pl.when(is_home)
        def _():
            to_near.start()
            to_next.start()

        for chunk in order:
            conv_chunk(chunk)

            @pl.when(is_home)
            def _(chunk=chunk):
                to_x(chunk).start()
                to_buddy(chunk).start()

            @pl.when(is_guest)
            def _(chunk=chunk):
                swap(chunk).start()

        @pl.when(is_guest)
        def _():
            to_swap.start()
            for chunk in (flip3(me), flip1(me), flip2(me), me):
                arrived(base_at, chunk)
                to_x(chunk).start()
                to_buddy(chunk).start()
            for k in range(2):
                teach_send(rows_of(0), near.at[k], (ring, me), 1 + k).wait_recv()
                at = me if k == 0 else flip1(me)

                def turn(i, _, k=k, at=at):
                    rows = pl.ds(pl.multiple_of(i * 128, 128), 128)
                    for c in range(0, stripe, 128):
                        cols = pl.ds(pl.multiple_of(at * stripe + c, 128), 128)
                        teach[rows, cols] = near[k, c : c + 128, rows].T
                    return 0

                lax.fori_loop(0, stripe // 128, turn, 0)

        for chunk in (base_at, flip2(base_at)):
            arrived(flip1(base_at), chunk)
            pass_on(chunk).start()
    else:
        for c in range(groups):
            conv_chunk(c)
        pl.semaphore_wait(barrier, greeted)

        def send_all(copy_do):
            def body(i, _):
                chunk, step = i // (groups - 1), 1 + lax.rem(i, groups - 1)
                copy_do(gather_copy(me, me, chunk, (ring, lax.rem(me + step, groups)), send_sem.at[step, chunk]))
                return 0

            lax.fori_loop(0, groups * (groups - 1), body, 0)

        send_all(lambda copy: copy.start())

    def wait_chunk(t, chunk):
        if paired:
            @pl.when(t >= 2)
            def _():
                arrived(flip1(base_at), chunk)
                pass_on(chunk).start()

            arrived(flip2(base_at), chunk)
            arrived(flip3(base_at), chunk)
        else:
            def body(step, _):
                arrived(lax.rem(me + step, groups), chunk)
                return 0

            lax.fori_loop(1, groups, body, 0)

    norm_tile = min(32, stripe)

    def scale_of(base):
        squares = jnp.zeros((norm_tile, width), f32)
        for g in range(groups):
            block = held[g, pl.ds(base, norm_tile)].astype(f32)
            squares = squares + block * block
        return lax.rsqrt(jnp.sum(squares, axis=1, keepdims=True) / full + epsilon)

    def normalize(chunk, dest):
        def body(i, _):
            base = pl.multiple_of(chunk * stripe + i * norm_tile, norm_tile)
            inverse = scale_of(base)
            for g in range(groups):
                block = held[g, pl.ds(base, norm_tile)].astype(f32)
                dest[pl.ds(pl.multiple_of(i * norm_tile, norm_tile), norm_tile), g * width : (g + 1) * width] = (
                    block * inverse
                ).astype(bf16)
            return 0

        lax.fori_loop(0, stripe // norm_tile, body, 0)

    if paired:
        pl.when(is_home)(teach_copy.wait)

        @pl.when(is_guest)
        def _():
            teach_send(far_in, teach.at[:, far_in], (ring, me), 0).wait_recv()
    else:
        teach_copy.wait()
    mat = min(256, stripe)

    def gram_chunk(t, _):
        if paired:
            late = jnp.where(t == 2, flip3(me), flip1(me))
            chunk = jnp.where(t == 0, base_at, jnp.where(t == 1, flip2(base_at), late))
        else:
            chunk = lax.rem(me + t, groups)
        wait_chunk(t, chunk)
        normalize(chunk, block_n)

        @pl.when(t == 0)
        def _():
            own_n[...] = block_n[...]

        def body(m, _):
            rows = pl.ds(pl.multiple_of(m * mat, mat), mat)
            similarity = lax.dot_general(
                own_n[rows], block_n[...], (((1,), (1,)), ((), ())), preferred_element_type=f32
            ) / full
            residue = (factor * (similarity - teach[rows, rows_of(chunk)])).astype(bf16)
            total[rows] += jnp.dot(residue, block_n[...], preferred_element_type=f32)
            return 0

        lax.fori_loop(0, stripe // mat, body, 0)
        return 0

    lax.fori_loop(0, groups, gram_chunk, 0)

    def finish(i, _):
        local = pl.multiple_of(i * norm_tile, norm_tile)
        base = pl.multiple_of(base_at * stripe + i * norm_tile, norm_tile)
        rows = pl.ds(local, norm_tile)
        inverse = scale_of(base)
        inner = jnp.zeros((norm_tile, width), f32)
        for g in range(groups):
            part = slice(g * width, (g + 1) * width)
            inner = inner + held[g, pl.ds(base, norm_tile)].astype(f32) * inverse * total[rows, part]
        projection = jnp.sum(inner, axis=1, keepdims=True) / full
        for g in range(groups):
            part = slice(g * width, (g + 1) * width)
            normed = held[g, pl.ds(base, norm_tile)].astype(f32) * inverse
            outgoing[g, rows] = (inverse * (total[rows, part] - normed * projection)).astype(bf16)
        return 0

    pieces = max(1, min(4, stripe // 128))
    piece = stripe // pieces
    steps = piece // norm_tile

    def exchange(target, p, source_row):
        return pltpu.make_async_remote_copy(
            src_ref=outgoing.at[target, pl.ds(p * piece, piece)],
            dst_ref=hgrad.at[rows_of(source_row, piece, p * piece)],
            send_sem=a2a_send.at[target, p], recv_sem=a2a_recv.at[source_row, p],
            device_id=(proc, target), device_id_type=MESH,
        )

    if paired:
        targets = (flip3(me), flip1(me), flip2(me))
    else:
        targets = tuple(lax.rem(me + groups - step, groups) for step in range(1, groups))

    def stay(p):
        hgrad[rows_of(base_at, piece, p * piece)] = outgoing[me, pl.ds(p * piece, piece)]

    for p in reversed(range(pieces)):
        lax.fori_loop(p * steps, (p + 1) * steps, finish, 0)
        for target in targets:
            exchange(target, p, base_at).start()
        if paired:
            @pl.when(is_guest)
            def _(p=p):
                exchange(me, p, base_at).start()

            @pl.when(is_home)
            def _(p=p):
                stay(p)
        else:
            stay(p)

    def back_tile(base):
        for k in range(0, width, 128):
            lane = slice(k, min(k + 128, width))
            up = hgrad[pl.ds(base, tile + PAD), lane].astype(f32)
            for b, (conv, raw, weights, store) in enumerate(
                ((conv_v, raw_g, filter_gate, gate_out), (conv_g, raw_v, filter_value, value_out))
            ):
                window = up * conv[pl.ds(base, tile + PAD), lane]
                signal = raw[pl.ds(pl.multiple_of(base + PAD, PAD), tile), lane].astype(f32)
                out = None
                for j in range(taps):
                    shifted = (window if j == 0 else pltpu.roll(window, tile + PAD - j, 0))[:tile]
                    term = weights[j : j + 1, lane] * shifted
                    out = term if out is None else out + term
                    product = shifted * signal
                    folded = product[0:8]
                    for r in range(8, tile, 8):
                        folded = folded + product[r : r + 8]
                    sums[b, j, :, lane] += folded
                store[0, pl.ds(base, tile), lane] = out.astype(bf16)

    tiles = stripe // tile
    per = tiles // pieces
    if paired:
        sources = (base_at, flip2(base_at), flip1(base_at), flip3(base_at))
    else:
        sources = tuple(lax.rem(me + step, groups) for step in range(groups))
    for p in reversed(range(pieces)):
        for step, source in enumerate(sources):
            def landed(p=p, source=source):
                exchange(source, p, source).wait_recv()

            if step:
                landed()
            elif paired:
                pl.when(is_guest)(landed)

            def inner_tiles(i, _, source=source):
                back_tile(pl.multiple_of(source * stripe + i * tile, tile))
                return 0

            lax.fori_loop(p * per, (p + 1) * per - (1 if p == pieces - 1 else 0), inner_tiles, 0)

    def last_tiles(c, _):
        back_tile(pl.multiple_of(c * stripe + (tiles - 1) * tile, tile))
        return 0

    lax.fori_loop(0, groups, last_tiles, 0)
    for b in range(2):
        for j in range(taps):
            mine[b, j : j + 1] = jnp.sum(sums[b, j], axis=0, keepdims=True)
        mine[b, taps:] = jnp.zeros((8 - taps, width), f32)

    def tap_copy(to, slot):
        return pltpu.make_async_remote_copy(
            src_ref=mine, dst_ref=others.at[slot], send_sem=tap_send.at[slot], recv_sem=tap_recv.at[slot],
            device_id=(to, me), device_id_type=MESH,
        )

    tap_copies = [tap_copy(lax.rem(ring + step, rings), step) for step in range(1, rings)]
    for copy in tap_copies:
        copy.start()
    summed = [mine[b] for b in range(2)]
    for step, copy in enumerate(tap_copies):
        copy.wait_recv()
        summed = [summed[b] + others[step + 1, b] for b in range(2)]
    gate_taps[...] = summed[0][:taps] * norm_factor
    value_taps[...] = summed[1][:taps] * norm_factor

    for copy in tap_copies:
        copy.wait_send()
    if paired:
        for chunk in range(groups):
            to_x(chunk).wait_send()
            to_buddy(chunk).wait_send()
            pass_on(chunk).wait_send()

        @pl.when(is_home)
        def _():
            to_near.wait_send()
            to_next.wait_send()

        @pl.when(is_guest)
        def _():
            to_swap.wait_send()
            for chunk in range(groups):
                swap(chunk).wait_send()
            for p in range(pieces):
                exchange(me, p, base_at).wait_send()
    else:
        send_all(lambda copy: copy.wait_send())
    for target in targets:
        for p in range(pieces):
            exchange(target, p, base_at).wait_send()


def on_device(gate_raw, value_raw, filter_gate, filter_value, teacher):
    seq_count, length, width = gate_raw.shape
    groups, rings = lax.axis_size("chan"), lax.axis_size("seq")
    taps = filter_gate.shape[0]
    stripe, full = length // groups, width * groups
    norm_factor = 1.0 / math.sqrt(rings * seq_count * length)
    f32, bf16 = jnp.float32, jnp.bfloat16
    any_space = pl.BlockSpec(memory_space=pl.ANY)
    vmem = pl.BlockSpec(memory_space=pltpu.VMEM)
    dma = pltpu.SemaphoreType.DMA
    return pl.pallas_call(
        functools.partial(kernel, groups, rings, taps, norm_factor),
        out_shape=(
            pltpu.VMEM(gate_raw.shape, bf16),
            pltpu.VMEM(gate_raw.shape, bf16),
            jax.ShapeDtypeStruct((taps, width), f32),
            jax.ShapeDtypeStruct((taps, width), f32),
        ),
        in_specs=[any_space, any_space, vmem, vmem, any_space],
        out_specs=(vmem, vmem, vmem, vmem),
        scratch_shapes=[
            pltpu.VMEM((length + PAD, width), bf16),
            pltpu.VMEM((length + PAD, width), bf16),
            pltpu.VMEM((length + PAD, width), f32),
            pltpu.VMEM((length + PAD, width), f32),
            pltpu.VMEM((groups + 1, length, width), bf16),
            pltpu.VMEM((stripe, length), f32),
            pltpu.VMEM((stripe, full), bf16),
            pltpu.VMEM((stripe, full), bf16),
            pltpu.VMEM((stripe, full), f32),
            pltpu.VMEM((groups, stripe, width), bf16),
            pltpu.VMEM((length + PAD, width), bf16),
            pltpu.VMEM((2, taps, 8, width), f32),
            pltpu.VMEM((2, 8, width), f32),
            pltpu.VMEM((rings, 2, 8, width), f32),
            dma((3, groups)),
            dma((groups, groups)),
            dma((groups, groups)),
            dma((groups, 4)),
            dma((groups, 4)),
            dma((rings,)),
            dma((rings,)),
            pltpu.VMEM((2, stripe, stripe), f32),
            dma((3,)),
            dma((3,)),
        ],
        compiler_params=pltpu.CompilerParams(
            collective_id=0, has_side_effects=True, vmem_limit_bytes=52 * 1024 * 1024
        ),
    )(gate_raw, value_raw, filter_gate, filter_value, teacher)


def solution(mesh):
    placed = (
        P("seq", None, "chan"),
        P("seq", None, "chan"),
        P(None, "chan"),
        P(None, "chan"),
        P("seq", "chan", None),
    )
    return jax.shard_map(
        on_device,
        mesh=mesh,
        in_specs=placed,
        out_specs=(
            P("seq", None, "chan"),
            P("seq", None, "chan"),
            P(None, "chan"),
            P(None, "chan"),
        ),
        check_vma=False,
    )
```

profile of v0, /device:TPU:0, one launch (start us, length us, event | category | flops | bytes accessed | tf_op | source)
XLA Modules:
  0.0 117.8 jit_solution(3129332646980985734)
XLA Ops:
  0.6 113.3 %shard_map.84 = (bf16[1,2048,512]{2,1,0:T(8,128)(2,1)S(1)}, bf16[1,2048,512]{2,1,0:T(8,128)(2,1)S(1)}, f32[7,512]{1,0:T(8,128)}, f32[7,512]{1,0:T(8,128)}) custom-call(bf16[1,2048,512]{2,1,0:T(8,128)(2,1)} %gate_in.1, bf16[1,2048,512]{2,1,0:T(8,128)(2,1)} %value_in.1, f32[7,512]{1,0:T(8,128)} %filter_gate.1, f32[7,512]{1,0:T(8,128)} %filter_value.1, ...), custom_call_target="tpu_custom_call" | custom-call | tf_op jit(solution)/shard_map/pallas_call | solution.py:430
  113.9 1.3 %copy.13 = bf16[1,2048,512]{2,1,0:T(8,128)(2,1)} copy(bf16[1,2048,512]{2,1,0:T(8,128)(2,1)S(1)} %get-tuple-element.4) | data formatting | bytes 4194304
  115.2 0.0 copy-start.1
  115.2 0.0 copy-start
  115.2 1.3 %copy.14 = bf16[1,2048,512]{2,1,0:T(8,128)(2,1)} copy(bf16[1,2048,512]{2,1,0:T(8,128)(2,1)S(1)} %get-tuple-element.5) | data formatting | bytes 4194304
  116.6 0.0 copy-done.1
  116.6 0.6 copy.15
  117.2 0.0 copy-done
  117.2 0.6 copy.16
Async XLA Ops:
  115.2 1.3 %copy-start.1 = (f32[7,512]{1,0:T(8,128)S(1)}, f32[7,512]{1,0:T(8,128)}, u32[]{:S(2)}) copy-start(f32[7,512]{1,0:T(8,128)} %get-tuple-element.14) | copy-start | bytes 43012
  115.2 1.9 %copy-start = (f32[7,512]{1,0:T(8,128)S(1)}, f32[7,512]{1,0:T(8,128)}, u32[]{:S(2)}) copy-start(f32[7,512]{1,0:T(8,128)} %get-tuple-element.15) | copy-start | bytes 43012
where the time goes:
time: 119 us; the launch traced here: 118 us
  Pallas kernels  113 us (95%)
  local copies, waits for them, and re-layouts  3.86 us (3%)
    pallas_call x1, Pallas kernels, on_device(): pl.pallas_call(functools.partial(kernel, groups, rings, taps, norm_factor...  113 us
    unnamed x8, local copies, waits for them, and re-layouts  3.86 us

commit v1 on v0

--- a/solution.py
+++ b/solution.py
@@ -11,17 +11,17 @@
 epsilon = 1e-06
 PAD = 16
 TILE = 64
+BLK = 256
 MESH = pl.DeviceIdType.MESH
 
 
-def kernel(
+def stripe_kernel(
     groups, rings, taps, norm_factor,
     gate_in, value_in, filter_gate, filter_value, teacher_in,
     gate_out, value_out, gate_taps, value_taps,
     raw_g, raw_v, conv_g, conv_v, held, teach, own_n, block_n, total, outgoing, hgrad,
     sums, mine, others,
     in_sem, send_sem, recv_sem, a2a_send, a2a_recv, tap_send, tap_recv,
-    near, teach_send_sem, teach_recv_sem,
 ):
     length, width = gate_in.shape[1:]
     stripe = length // groups
@@ -31,21 +31,7 @@
     lanes = [slice(k, min(k + 128, width)) for k in range(0, width, 128)]
     f32, bf16 = jnp.float32, jnp.bfloat16
     me, ring = lax.axis_index("chan"), lax.axis_index("seq")
-    paired = groups == 4 and rings % 2 == 0
-    flip1 = lambda at: at + 1 - 2 * lax.rem(at, 2)
-    flip2 = lambda at: lax.rem(at + 2, 4)
-    flip3 = lambda at: 3 - at
-    if paired:
-        core = lax.rem(ring, 2)
-        buddy = ring + 1 - 2 * core
-        side = me // 2
-        same = 1 - (core - side) * (core - side)
-        base_at = same * me + (1 - same) * flip2(me)
-        slot = same * me + (1 - same) * groups
-        proc = ring - core + side
-        is_home, is_guest = same == 1, same == 0
-    else:
-        base_at, slot, proc = me, me, ring
+    base_at, slot, proc = me, me, ring
 
     def rows_of(chunk, size=stripe, start=0):
         return pl.ds(pl.multiple_of(chunk * stripe + start, math.gcd(stripe, start) if start else stripe), size)
@@ -59,17 +45,12 @@
     for copy in in_copies:
         copy.start()
     teach_copy = pltpu.make_async_copy(teacher_in.at[0], teach, in_sem.at[2, 0])
-    if paired:
-        pl.when(is_home)(teach_copy.start)
-    else:
-        teach_copy.start()
+    teach_copy.start()
 
     barrier = pltpu.get_barrier_semaphore()
     for step in range(1, groups):
         pl.semaphore_signal(barrier, inc=1, device_id=(ring, lax.rem(me + step, groups)), device_id_type=MESH)
-        if paired:
-            pl.semaphore_signal(barrier, inc=1, device_id=(buddy, lax.rem(me + step, groups)), device_id_type=MESH)
-    greeted = (groups - 1) * (2 if paired else 1) + rings - 1
+    greeted = groups + rings - 2
     for step in range(1, rings):
         pl.semaphore_signal(barrier, inc=1, device_id=(lax.rem(ring + step, rings), me), device_id_type=MESH)
 
@@ -111,105 +92,26 @@
     def arrived(source, chunk):
         gather_copy(source, source, chunk, (ring, me), send_sem.at[0, 0]).wait_recv()
 
-    if paired:
-        far = pl.ds(pl.multiple_of(side * 2 * stripe, stripe), 2 * stripe)
-
-        def teach_send(cols, dst, to, k):
-            return pltpu.make_async_remote_copy(
-                src_ref=teacher_in.at[0, :, cols], dst_ref=dst, send_sem=teach_send_sem.at[k],
-                recv_sem=teach_recv_sem.at[k], device_id=to, device_id_type=MESH,
-            )
-
-        to_swap = teach_send(far, teach.at[:, far], (buddy, flip2(me)), 0)
-        to_near = teach_send(rows_of(flip2(me)), near.at[0], (buddy, me), 1)
-        to_next = teach_send(rows_of(flip3(me)), near.at[1], (buddy, flip1(me)), 2)
-        far_in = pl.ds(pl.multiple_of((1 - side) * 2 * stripe, stripe), 2 * stripe)
-
-        def to_x(chunk):
-            return gather_copy(base_at, base_at, chunk, (ring, flip1(me)), send_sem.at[0, chunk])
-
-        def to_buddy(chunk):
-            return gather_copy(base_at, base_at, chunk, (buddy, me), send_sem.at[1, chunk])
-
-        def pass_on(chunk):
-            return gather_copy(flip1(base_at), flip1(base_at), chunk, (buddy, me), send_sem.at[2, chunk])
-
-        def swap(chunk):
-            return gather_copy(groups, me, chunk, (buddy, flip2(me)), send_sem.at[3, chunk])
-
-        order = (flip1(me), flip3(me), me, flip2(me))
-        pl.semaphore_wait(barrier, greeted)
-
-        @pl.when(is_home)
-        def _():
-            to_near.start()
-            to_next.start()
-
-        for chunk in order:
-            conv_chunk(chunk)
-
-            @pl.when(is_home)
-            def _(chunk=chunk):
-                to_x(chunk).start()
-                to_buddy(chunk).start()
-
-            @pl.when(is_guest)
-            def _(chunk=chunk):
-                swap(chunk).start()
-
-        @pl.when(is_guest)
-        def _():
-            to_swap.start()
-            for chunk in (flip3(me), flip1(me), flip2(me), me):
-                arrived(base_at, chunk)
-                to_x(chunk).start()
-                to_buddy(chunk).start()
-            for k in range(2):
-                teach_send(rows_of(0), near.at[k], (ring, me), 1 + k).wait_recv()
-                at = me if k == 0 else flip1(me)
-
-                def turn(i, _, k=k, at=at):
-                    rows = pl.ds(pl.multiple_of(i * 128, 128), 128)
-                    for c in range(0, stripe, 128):
-                        cols = pl.ds(pl.multiple_of(at * stripe + c, 128), 128)
-                        teach[rows, cols] = near[k, c : c + 128, rows].T
-                    return 0
-
-                lax.fori_loop(0, stripe // 128, turn, 0)
-
-        for chunk in (base_at, flip2(base_at)):
-            arrived(flip1(base_at), chunk)
-            pass_on(chunk).start()
-    else:
-        for c in range(groups):
-            conv_chunk(c)
-        pl.semaphore_wait(barrier, greeted)
-
-        def send_all(copy_do):
-            def body(i, _):
-                chunk, step = i // (groups - 1), 1 + lax.rem(i, groups - 1)
-                copy_do(gather_copy(me, me, chunk, (ring, lax.rem(me + step, groups)), send_sem.at[step, chunk]))
-                return 0
-
-            lax.fori_loop(0, groups * (groups - 1), body, 0)
-
-        send_all(lambda copy: copy.start())
-
-    def wait_chunk(t, chunk):
-        if paired:
-            @pl.when(t >= 2)
-            def _():
-                arrived(flip1(base_at), chunk)
-                pass_on(chunk).start()
-
-            arrived(flip2(base_at), chunk)
-            arrived(flip3(base_at), chunk)
-        else:
-            def body(step, _):
-                arrived(lax.rem(me + step, groups), chunk)
-                return 0
-
-            lax.fori_loop(1, groups, body, 0)
+    for c in range(groups):
+        conv_chunk(c)
+    pl.semaphore_wait(barrier, greeted)
+
+    def send_all(copy_do):
+        def body(i, _):
+            chunk, step = i // (groups - 1), 1 + lax.rem(i, groups - 1)
+            copy_do(gather_copy(me, me, chunk, (ring, lax.rem(me + step, groups)), send_sem.at[step, chunk]))
+            return 0
+
+        lax.fori_loop(0, groups * (groups - 1), body, 0)
+
+    send_all(lambda copy: copy.start())
+
+    def wait_chunk(chunk):
+        def body(step, _):
+            arrived(lax.rem(me + step, groups), chunk)
+            return 0
+
+        lax.fori_loop(1, groups, body, 0)
 
     norm_tile = min(32, stripe)
 
@@ -233,23 +135,12 @@
 
         lax.fori_loop(0, stripe // norm_tile, body, 0)
 
-    if paired:
-        pl.when(is_home)(teach_copy.wait)
-
-        @pl.when(is_guest)
-        def _():
-            teach_send(far_in, teach.at[:, far_in], (ring, me), 0).wait_recv()
-    else:
-        teach_copy.wait()
+    teach_copy.wait()
     mat = min(256, stripe)
 
     def gram_chunk(t, _):
-        if paired:
-            late = jnp.where(t == 2, flip3(me), flip1(me))
-            chunk = jnp.where(t == 0, base_at, jnp.where(t == 1, flip2(base_at), late))
-        else:
-            chunk = lax.rem(me + t, groups)
-        wait_chunk(t, chunk)
+        chunk = lax.rem(me + t, groups)
+        wait_chunk(chunk)
         normalize(chunk, block_n)
 
         @pl.when(t == 0)
@@ -298,10 +189,7 @@
             device_id=(proc, target), device_id_type=MESH,
         )
 
-    if paired:
-        targets = (flip3(me), flip1(me), flip2(me))
-    else:
-        targets = tuple(lax.rem(me + groups - step, groups) for step in range(1, groups))
+    targets = tuple(lax.rem(me + groups - step, groups) for step in range(1, groups))
 
     def stay(p):
         hgrad[rows_of(base_at, piece, p * piece)] = outgoing[me, pl.ds(p * piece, piece)]
@@ -310,16 +198,7 @@
         lax.fori_loop(p * steps, (p + 1) * steps, finish, 0)
         for target in targets:
             exchange(target, p, base_at).start()
-        if paired:
-            @pl.when(is_guest)
-            def _(p=p):
-                exchange(me, p, base_at).start()
-
-            @pl.when(is_home)
-            def _(p=p):
-                stay(p)
-        else:
-            stay(p)
+        stay(p)
 
     def back_tile(base):
         for k in range(0, width, 128):
@@ -344,10 +223,7 @@
 
     tiles = stripe // tile
     per = tiles // pieces
-    if paired:
-        sources = (base_at, flip2(base_at), flip1(base_at), flip3(base_at))
-    else:
-        sources = tuple(lax.rem(me + step, groups) for step in range(groups))
+    sources = tuple(lax.rem(me + step, groups) for step in range(groups))
     for p in reversed(range(pieces)):
         for step, source in enumerate(sources):
             def landed(p=p, source=source):
@@ -355,8 +231,6 @@
 
             if step:
                 landed()
-            elif paired:
-                pl.when(is_guest)(landed)
 
             def inner_tiles(i, _, source=source):
                 back_tile(pl.multiple_of(source * stripe + i * tile, tile))
@@ -392,32 +266,410 @@
 
     for copy in tap_copies:
         copy.wait_send()
-    if paired:
-        for chunk in range(groups):
-            to_x(chunk).wait_send()
-            to_buddy(chunk).wait_send()
-            pass_on(chunk).wait_send()
-
-        @pl.when(is_home)
-        def _():
-            to_near.wait_send()
-            to_next.wait_send()
-
-        @pl.when(is_guest)
-        def _():
-            to_swap.wait_send()
-            for chunk in range(groups):
-                swap(chunk).wait_send()
-            for p in range(pieces):
-                exchange(me, p, base_at).wait_send()
-    else:
-        send_all(lambda copy: copy.wait_send())
+    send_all(lambda copy: copy.wait_send())
     for target in targets:
         for p in range(pieces):
             exchange(target, p, base_at).wait_send()
 
 
-def on_device(gate_raw, value_raw, filter_gate, filter_value, teacher):
+def quad_kernel(
+    rings, taps, norm_factor,
+    gate_in, value_in, filter_gate, filter_value, teacher_in,
+    gate_out, value_out, gate_taps, value_taps,
+    raw_g, raw_v, conv_g, conv_v, hid, nrm, teach, perm, keep,
+    s1, r1, s2, r2, res, gbuf, hgrad, lane_sums, small, invc,
+    sums, mine, others,
+    in_sem, s1_send, s1_recv, s2_send, s2_recv, ag_send, ag_recv,
+    small_send, small_recv, tap_send, tap_recv,
+):
+    groups = 4
+    length, width = gate_in.shape[1:]
+    stripe, full = length // groups, width * groups
+    factor = 16.0 / math.sqrt(length)
+    blocks = length // BLK
+    half, quarter, eighth = BLK // 2, BLK // 4, BLK // 8
+    lanes = [slice(k, k + 128) for k in range(0, width, 128)]
+    f32, bf16 = jnp.float32, jnp.bfloat16
+    me, ring = lax.axis_index("chan"), lax.axis_index("seq")
+    x, y = lax.rem(me, 2), me // 2
+    across, along, diagonal = me + 1 - 2 * x, lax.rem(me + 2, 4), 3 - me
+    offset = [BLK * (l * (l + 1) // 2) for l in range(blocks)]
+
+    def rows(start, size, unit=None):
+        return pl.ds(pl.multiple_of(start, unit or size), size)
+
+    def push(src, dst, send, recv, to):
+        return pltpu.make_async_remote_copy(
+            src_ref=src, dst_ref=dst, send_sem=send, recv_sem=recv,
+            device_id=(ring, to), device_id_type=MESH,
+        )
+
+    in_copies = []
+    for l in range(blocks):
+        for k, (src, dst) in enumerate(((gate_in, raw_g), (value_in, raw_v))):
+            in_copies.append(pltpu.make_async_copy(
+                src.at[0, pl.ds(l * BLK, BLK)], dst.at[pl.ds(PAD + l * BLK, BLK)], in_sem.at[k, l]
+            ))
+    for copy in in_copies:
+        copy.start()
+    teach_copy = pltpu.make_async_copy(teacher_in.at[0], teach, in_sem.at[2, 0])
+    teach_copy.start()
+
+    barrier = pltpu.get_barrier_semaphore()
+    for to in (across, along, diagonal):
+        pl.semaphore_signal(barrier, inc=1, device_id=(ring, to), device_id_type=MESH)
+    for step in range(1, rings):
+        pl.semaphore_signal(barrier, inc=1, device_id=(lax.rem(ring + step, rings), me), device_id_type=MESH)
+
+    raw_g[0:PAD] = jnp.zeros((PAD, width), bf16)
+    raw_v[0:PAD] = jnp.zeros((PAD, width), bf16)
+    conv_g[length:] = jnp.zeros((PAD, width), f32)
+    conv_v[length:] = jnp.zeros((PAD, width), f32)
+    hgrad[length:] = jnp.zeros((PAD, width), f32)
+    sums[...] = jnp.zeros(sums.shape, f32)
+
+    def share(kind, l):
+        small[kind, me, l] = jnp.broadcast_to(jnp.sum(lane_sums[...].T, axis=0, keepdims=True), (8, BLK))
+        for k, to in enumerate((across, along, diagonal)):
+            here = small.at[kind, me, l]
+            push(here, here, small_send.at[kind, k, l], small_recv.at[kind, me, l], to).start()
+
+    def total(kind, l):
+        for o in (across, along, diagonal):
+            there = small.at[kind, o, l]
+            push(there, there, small_send.at[kind, 0, l], small_recv.at[kind, o, l], o).wait_recv()
+        return small[kind, 0, l, 0:1] + small[kind, 1, l, 0:1] + small[kind, 2, l, 0:1] + small[kind, 3, l, 0:1]
+
+    def column(row):
+        return jnp.broadcast_to(row, (128, BLK)).T
+
+    def conv(l):
+        in_copies[2 * l].wait()
+        in_copies[2 * l + 1].wait()
+
+        def body(i, _):
+            base = pl.multiple_of(l * BLK + i * TILE, TILE)
+            squares = jnp.zeros((TILE, 128), f32)
+            for lane in lanes:
+                made = []
+                for raw, weights, store in ((raw_g, filter_gate, conv_g), (raw_v, filter_value, conv_v)):
+                    window = raw[pl.ds(base, TILE + PAD), lane].astype(f32)
+                    out = weights[0:1, lane] * window[PAD:]
+                    for j in range(1, taps):
+                        out = out + weights[j : j + 1, lane] * pltpu.roll(window, j, 0)[PAD:]
+                    store[pl.ds(base, TILE), lane] = out
+                    made.append(out)
+                hidden = (made[0] * made[1]).astype(bf16)
+                hid[pl.ds(base, TILE), lane] = hidden
+                hidden = hidden.astype(f32)
+                squares = squares + hidden * hidden
+            lane_sums[pl.ds(pl.multiple_of(i * TILE, TILE), TILE)] = squares
+            return 0
+
+        lax.fori_loop(0, BLK // TILE, body, 0)
+
+    def normalize(l):
+        invc[pl.ds(l * BLK, BLK)] = column(lax.rsqrt(total(0, l) / full + epsilon))
+
+        def body(i, _):
+            base = pl.multiple_of(l * BLK + i * TILE, TILE)
+            inverse = invc[pl.ds(base, TILE)]
+            for lane in lanes:
+                nrm[pl.ds(base, TILE), lane] = (hid[pl.ds(base, TILE), lane].astype(f32) * inverse).astype(bf16)
+            return 0
+
+        lax.fori_loop(0, BLK // TILE, body, 0)
+
+    pieces = (quarter * (1 - x), half + quarter * (1 - y), quarter * x, half + quarter * y)
+
+    def stage_one(l):
+        span = pl.ds(offset[l], (l + 1) * BLK)
+        for k, to in enumerate((across, along)):
+            yield push(s1.at[k, :, span], r1.at[k, :, span], s1_send.at[k, l], s1_recv.at[k, l], to)
+
+    def stage_two(l):
+        span = pl.ds(offset[l], (l + 1) * BLK)
+        for k, to in enumerate((across, along)):
+            yield push(s2.at[k, :, span], r2.at[k, :, span], s2_send.at[k, l], s2_recv.at[k, l], to)
+
+    def gram(l):
+        for k, piece in enumerate(pieces):
+            perm[k * quarter : (k + 1) * quarter] = nrm[rows(l * BLK + piece, quarter)]
+        top = (l * BLK) % stripe
+        held = jnp.where(me == (l * BLK) // stripe, 1.0, 0.0)
+
+        def body(j, _):
+            part = lax.dot_general(
+                perm[...], nrm[rows(j * BLK, BLK)], (((1,), (1,)), ((), ())), preferred_element_type=f32
+            ) / full
+            cols = rows(offset[l] + j * BLK, BLK)
+            for k, piece in enumerate(pieces):
+                target = teach[rows(top + piece, quarter), rows(j * BLK, BLK)]
+                apart = part[k * quarter : (k + 1) * quarter] - held * target
+                if k < 2:
+                    s1[k, :, cols] = apart.astype(bf16)
+                else:
+                    keep[k - 2, :, cols] = apart
+            return 0
+
+        lax.fori_loop(0, l + 1, body, 0)
+        for copy in stage_one(l):
+            copy.start()
+
+    turns = ((0, y), (1, x))
+
+    def combine(l):
+        for copy in stage_one(l):
+            copy.wait_recv()
+
+        def body(j, _):
+            cols = rows(offset[l] + j * BLK, BLK)
+            for k, own in turns:
+                away = rows(eighth * (1 - own), eighth)
+                s2[1 - k, :, cols] = (keep[k, away, cols] + r1[k, away, cols].astype(f32)).astype(bf16)
+            return 0
+
+        lax.fori_loop(0, l + 1, body, 0)
+        for copy in stage_two(l):
+            copy.start()
+
+    def place(l, k, px, py):
+        return l * BLK + (quarter * px + eighth * py if k == 0 else half + quarter * py + eighth * px)
+
+    def residue(l):
+        for copy in stage_two(l):
+            copy.wait_recv()
+
+        def body(j, _):
+            cols = rows(offset[l] + j * BLK, BLK)
+            for k, own in turns:
+                here = rows(eighth * own, eighth)
+                apart = keep[k, here, cols] + r1[k, here, cols].astype(f32) + r2[1 - k, :, cols].astype(f32)
+                res[rows(place(l, k, x, y), eighth), rows(j * BLK, BLK)] = (factor * apart).astype(bf16)
+            return 0
+
+        lax.fori_loop(0, l + 1, body, 0)
+
+    def gather(l, slot, k, px, py, to):
+        area = res.at[rows(place(l, k, px, py), eighth), pl.ds(0, (l + 1) * BLK)]
+        return push(area, area, ag_send.at[slot, l], ag_recv.at[slot, l], to)
+
+    def own_rows(l):
+        return (
+            gather(l, 0, 0, x, y, across), gather(l, 3, 1, x, y, along),
+            gather(l, 1, 1, x, y, across), gather(l, 2, 0, x, y, along),
+        )
+
+    def relays(l):
+        return gather(l, 4, 0, 1 - x, y, along), gather(l, 5, 1, x, 1 - y, across)
+
+    def relay(l):
+        first, second = relays(l)
+        gather(l, 0, 0, 1 - x, y, across).wait_recv()
+        first.start()
+        gather(l, 3, 1, x, 1 - y, along).wait_recv()
+        second.start()
+
+    def landed(l):
+        gather(l, 1, 1, 1 - x, y, across).wait_recv()
+        gather(l, 2, 0, x, 1 - y, along).wait_recv()
+        gather(l, 4, 0, 1 - x, 1 - y, along).wait_recv()
+        gather(l, 5, 1, 1 - x, 1 - y, across).wait_recv()
+
+    def multiply(l):
+        start, stop = l * BLK, (l + 1) * BLK
+        out = jnp.dot(res[start:stop, 0:stop], nrm[0:stop], preferred_element_type=f32)
+        if stop < length:
+            out = out + lax.dot_general(
+                res[stop:length, start:stop], nrm[stop:length], (((0,), (0,)), ((), ())), preferred_element_type=f32
+            )
+        gbuf[l % 2] = out
+
+        def body(i, _):
+            local = rows(i * TILE, TILE)
+            at = rows(start + i * TILE, TILE)
+            inner = jnp.zeros((TILE, 128), f32)
+            for lane in lanes:
+                inner = inner + hid[at, lane].astype(f32) * invc[at] * gbuf[l % 2, local, lane]
+            lane_sums[local] = inner
+            return 0
+
+        lax.fori_loop(0, BLK // TILE, body, 0)
+        share(1, l)
+
+    def finish(l):
+        lane_sums[...] = column(total(1, l) / full)
+
+        def body(i, _):
+            local = rows(i * TILE, TILE)
+            at = rows(l * BLK + i * TILE, TILE)
+            inverse, projection = invc[at], lane_sums[local]
+            for lane in lanes:
+                normed = hid[at, lane].astype(f32) * inverse
+                hgrad[at, lane] = inverse * (gbuf[l % 2, local, lane] - normed * projection)
+            return 0
+
+        lax.fori_loop(0, BLK // TILE, body, 0)
+
+    def back(l):
+        def body(i, _):
+            base = pl.multiple_of(l * BLK + i * TILE, TILE)
+            for lane in lanes:
+                up = hgrad[pl.ds(base, TILE + PAD), lane]
+                for b, (conv_by, raw, weights, store) in enumerate(
+                    ((conv_v, raw_g, filter_gate, gate_out), (conv_g, raw_v, filter_value, value_out))
+                ):
+                    window = up * conv_by[pl.ds(base, TILE + PAD), lane]
+                    signal = raw[pl.ds(pl.multiple_of(base + PAD, PAD), TILE), lane].astype(f32)
+                    out = None
+                    for j in range(taps):
+                        shifted = (window if j == 0 else pltpu.roll(window, TILE + PAD - j, 0))[:TILE]
+                        term = weights[j : j + 1, lane] * shifted
+                        out = term if out is None else out + term
+                        product = shifted * signal
+                        folded = product[0:8]
+                        for r in range(8, TILE, 8):
+                            folded = folded + product[r : r + 8]
+                        sums[b, j, :, lane] += folded
+                    store[0, pl.ds(base, TILE), lane] = out.astype(bf16)
+            return 0
+
+        lax.fori_loop(0, BLK // TILE, body, 0)
+
+    order = ([blocks - 2, blocks - 1] + list(range(blocks - 3, -1, -1))) if blocks > 1 else [0]
+    conv(0)
+    pl.semaphore_wait(barrier, groups + rings - 2)
+    share(0, 0)
+    lag = 3
+    for t in range(1, blocks + lag + 2):
+        if t < blocks:
+            conv(t)
+            share(0, t)
+        if t == lag:
+            teach_copy.wait()
+        if 0 <= t - lag < blocks:
+            normalize(t - lag)
+            gram(t - lag)
+        if 0 <= t - lag - 1 < blocks:
+            combine(t - lag - 1)
+        if 0 <= t - lag - 2 < blocks:
+            l = t - lag - 2
+            residue(l)
+            if l in order[:2]:
+                for copy in own_rows(l):
+                    copy.start()
+    ready = []
+    for i, l in enumerate(order):
+        relay(l)
+        if i + 2 < blocks:
+            for copy in own_rows(order[i + 2]):
+                copy.start()
+        landed(l)
+        fresh = [] if i == 0 and blocks > 1 else ([blocks - 1, blocks - 2] if i == 1 else [l])
+        for at in fresh:
+            multiply(at)
+            ready.append(at)
+            if len(ready) > 1:
+                done = ready.pop(0)
+                finish(done)
+                back(done)
+    finish(ready[0])
+    back(ready[0])
+
+    for b in range(2):
+        for j in range(taps):
+            mine[b, j : j + 1] = jnp.sum(sums[b, j], axis=0, keepdims=True)
+        mine[b, taps:] = jnp.zeros((8 - taps, width), f32)
+
+    tap_copies = [
+        pltpu.make_async_remote_copy(
+            src_ref=mine, dst_ref=others.at[step], send_sem=tap_send.at[step], recv_sem=tap_recv.at[step],
+            device_id=(lax.rem(ring + step, rings), me), device_id_type=MESH,
+        )
+        for step in range(1, rings)
+    ]
+    for copy in tap_copies:
+        copy.start()
+    for l in range(blocks):
+        for copy in (*stage_one(l), *stage_two(l), *own_rows(l), *relays(l)):
+            copy.wait_send()
+        for kind in range(2):
+            for k, to in enumerate((across, along, diagonal)):
+                here = small.at[kind, me, l]
+                push(here, here, small_send.at[kind, k, l], small_recv.at[kind, me, l], to).wait_send()
+    summed = [mine[b] for b in range(2)]
+    for step, copy in enumerate(tap_copies):
+        copy.wait_recv()
+        summed = [summed[b] + others[step + 1, b] for b in range(2)]
+    gate_taps[...] = summed[0][:taps] * norm_factor
+    value_taps[...] = summed[1][:taps] * norm_factor
+    for copy in tap_copies:
+        copy.wait_send()
+
+
+def quad_call(gate_raw, value_raw, filter_gate, filter_value, teacher):
+    length, width = gate_raw.shape[1:]
+    rings = lax.axis_size("seq")
+    taps = filter_gate.shape[0]
+    stripe, blocks = length // 4, length // BLK
+    triangle = BLK * (blocks * (blocks + 1) // 2)
+    norm_factor = 1.0 / math.sqrt(rings * length)
+    f32, bf16 = jnp.float32, jnp.bfloat16
+    any_space = pl.BlockSpec(memory_space=pl.ANY)
+    vmem = pl.BlockSpec(memory_space=pltpu.VMEM)
+    dma = pltpu.SemaphoreType.DMA
+    return pl.pallas_call(
+        functools.partial(quad_kernel, rings, taps, norm_factor),
+        out_shape=(
+            pltpu.VMEM(gate_raw.shape, bf16),
+            pltpu.VMEM(gate_raw.shape, bf16),
+            jax.ShapeDtypeStruct((taps, width), f32),
+            jax.ShapeDtypeStruct((taps, width), f32),
+        ),
+        in_specs=[any_space, any_space, vmem, vmem, any_space],
+        out_specs=(vmem, vmem, vmem, vmem),
+        scratch_shapes=[
+            pltpu.VMEM((length + PAD, width), bf16),
+            pltpu.VMEM((length + PAD, width), bf16),
+            pltpu.VMEM((length + PAD, width), f32),
+            pltpu.VMEM((length + PAD, width), f32),
+            pltpu.VMEM((length, width), bf16),
+            pltpu.VMEM((length, width), bf16),
+            pltpu.VMEM((stripe, length), f32),
+            pltpu.VMEM((BLK, width), bf16),
+            pltpu.VMEM((2, BLK // 4, triangle), f32),
+            pltpu.VMEM((2, BLK // 4, triangle), bf16),
+            pltpu.VMEM((2, BLK // 4, triangle), bf16),
+            pltpu.VMEM((2, BLK // 8, triangle), bf16),
+            pltpu.VMEM((2, BLK // 8, triangle), bf16),
+            pltpu.VMEM((length, length), bf16),
+            pltpu.VMEM((2, BLK, width), f32),
+            pltpu.VMEM((length + PAD, width), f32),
+            pltpu.VMEM((BLK, 128), f32),
+            pltpu.VMEM((2, 4, blocks, 8, BLK), f32),
+            pltpu.VMEM((length, 128), f32),
+            pltpu.VMEM((2, taps, 8, width), f32),
+            pltpu.VMEM((2, 8, width), f32),
+            pltpu.VMEM((rings, 2, 8, width), f32),
+            dma((3, blocks)),
+            dma((2, blocks)),
+            dma((2, blocks)),
+            dma((2, blocks)),
+            dma((2, blocks)),
+            dma((6, blocks)),
+            dma((6, blocks)),
+            dma((2, 3, blocks)),
+            dma((2, 4, blocks)),
+            dma((rings,)),
+            dma((rings,)),
+        ],
+        compiler_params=pltpu.CompilerParams(
+            collective_id=0, has_side_effects=True, vmem_limit_bytes=58 * 1024 * 1024
+        ),
+    )(gate_raw, value_raw, filter_gate, filter_value, teacher)
+
+
+def stripe_call(gate_raw, value_raw, filter_gate, filter_value, teacher):
     seq_count, length, width = gate_raw.shape
     groups, rings = lax.axis_size("chan"), lax.axis_size("seq")
     taps = filter_gate.shape[0]
@@ -428,7 +680,7 @@
     vmem = pl.BlockSpec(memory_space=pltpu.VMEM)
     dma = pltpu.SemaphoreType.DMA
     return pl.pallas_call(
-        functools.partial(kernel, groups, rings, taps, norm_factor),
+        functools.partial(stripe_kernel, groups, rings, taps, norm_factor),
         out_shape=(
             pltpu.VMEM(gate_raw.shape, bf16),
             pltpu.VMEM(gate_raw.shape, bf16),
@@ -459,14 +711,19 @@
             dma((groups, 4)),
             dma((rings,)),
             dma((rings,)),
-            pltpu.VMEM((2, stripe, stripe), f32),
-            dma((3,)),
-            dma((3,)),
         ],
         compiler_params=pltpu.CompilerParams(
             collective_id=0, has_side_effects=True, vmem_limit_bytes=52 * 1024 * 1024
         ),
     )(gate_raw, value_raw, filter_gate, filter_value, teacher)
+
+
+def on_device(gate_raw, value_raw, filter_gate, filter_value, teacher):
+    length, width = gate_raw.shape[1:]
+    groups = lax.axis_size("chan")
+    square = groups == 4 and gate_raw.shape[0] == 1 and (length // 4) % BLK == 0 and width % 128 == 0
+    call = quad_call if square else stripe_call
+    return call(gate_raw, value_raw, filter_gate, filter_value, teacher)
 
 
 def solution(mesh):

time: 119 us -> 131 us (1.10)
  Pallas kernels: 113 us -> 126 us
    pallas_call x1, Pallas kernels: 113 us -> 126 us  [quad_call(): pl.pallas_call(functools.partial(quad_kernel, rings, taps, norm_factor),...]
where the time goes in v1:
time: 131 us
  Pallas kernels  126 us (96%)
  local copies, waits for them, and re-layouts  3.86 us (3%)
    pallas_call x1, Pallas kernels, quad_call(): pl.pallas_call(functools.partial(quad_kernel, rings, taps, norm_factor),...  126 us
    unnamed x8, local copies, waits for them, and re-layouts  3.86 us

profile of v1, /device:TPU:0, one launch (start us, length us, event | category | flops | bytes accessed | tf_op | source)
XLA Modules:
  0.0 130.9 jit_solution(14517809842998458144)
XLA Ops:
  0.6 126.4 %shard_map.84 = (bf16[1,2048,512]{2,1,0:T(8,128)(2,1)S(1)}, bf16[1,2048,512]{2,1,0:T(8,128)(2,1)S(1)}, f32[7,512]{1,0:T(8,128)}, f32[7,512]{1,0:T(8,128)}) custom-call(bf16[1,2048,512]{2,1,0:T(8,128)(2,1)} %gate_in.1, bf16[1,2048,512]{2,1,0:T(8,128)(2,1)} %value_in.1, f32[7,512]{1,0:T(8,128)} %filter_gate.1, f32[7,512]{1,0:T(8,128)} %filter_value.1, ...), custom_call_target="tpu_custom_call" | custom-call | tf_op jit(solution)/shard_map/pallas_call | solution.py:621
  127.0 1.3 %copy.13 = bf16[1,2048,512]{2,1,0:T(8,128)(2,1)} copy(bf16[1,2048,512]{2,1,0:T(8,128)(2,1)S(1)} %get-tuple-element.4) | data formatting | bytes 4194304
  128.3 0.0 copy-start.1
  128.4 0.0 copy-start
  128.4 1.3 %copy.14 = bf16[1,2048,512]{2,1,0:T(8,128)(2,1)} copy(bf16[1,2048,512]{2,1,0:T(8,128)(2,1)S(1)} %get-tuple-element.5) | data formatting | bytes 4194304
  129.7 0.0 copy-done.1
  129.7 0.6 copy.15
  130.3 0.0 copy-done
  130.3 0.6 copy.16
Async XLA Ops:
  128.3 1.3 %copy-start.1 = (f32[7,512]{1,0:T(8,128)S(1)}, f32[7,512]{1,0:T(8,128)}, u32[]{:S(2)}) copy-start(f32[7,512]{1,0:T(8,128)} %get-tuple-element.14) | copy-start | bytes 43012
  128.4 1.9 %copy-start = (f32[7,512]{1,0:T(8,128)S(1)}, f32[7,512]{1,0:T(8,128)}, u32[]{:S(2)}) copy-start(f32[7,512]{1,0:T(8,128)} %get-tuple-element.15) | copy-start | bytes 43012

commit v2 on v1

--- a/solution.py
+++ b/solution.py
@@ -382,14 +382,17 @@
 
     pieces = (quarter * (1 - x), half + quarter * (1 - y), quarter * x, half + quarter * y)
 
+    def reach(l, k):
+        return l * BLK + (half if k == 0 else BLK)
+
     def stage_one(l):
-        span = pl.ds(offset[l], (l + 1) * BLK)
         for k, to in enumerate((across, along)):
+            span = pl.ds(offset[l], reach(l, k))
             yield push(s1.at[k, :, span], r1.at[k, :, span], s1_send.at[k, l], s1_recv.at[k, l], to)
 
     def stage_two(l):
-        span = pl.ds(offset[l], (l + 1) * BLK)
         for k, to in enumerate((across, along)):
+            span = pl.ds(offset[l], reach(l, 1 - k))
             yield push(s2.at[k, :, span], r2.at[k, :, span], s2_send.at[k, l], s2_recv.at[k, l], to)
 
     def gram(l):
@@ -422,14 +425,18 @@
         for copy in stage_one(l):
             copy.wait_recv()
 
+        def add(k, own, cols):
+            away = rows(eighth * (1 - own), eighth)
+            s2[1 - k, :, cols] = (keep[k, away, cols] + r1[k, away, cols].astype(f32)).astype(bf16)
+
         def body(j, _):
-            cols = rows(offset[l] + j * BLK, BLK)
             for k, own in turns:
-                away = rows(eighth * (1 - own), eighth)
-                s2[1 - k, :, cols] = (keep[k, away, cols] + r1[k, away, cols].astype(f32)).astype(bf16)
-            return 0
-
-        lax.fori_loop(0, l + 1, body, 0)
+                add(k, own, rows(offset[l] + j * BLK, BLK))
+            return 0
+
+        lax.fori_loop(0, l, body, 0)
+        for k, own in turns:
+            add(k, own, pl.ds(offset[l] + l * BLK, half if k == 0 else BLK))
         for copy in stage_two(l):
             copy.start()
 
@@ -440,18 +447,23 @@
         for copy in stage_two(l):
             copy.wait_recv()
 
+        def add(k, own, cols, dest):
+            here = rows(eighth * own, eighth)
+            apart = keep[k, here, cols] + r1[k, here, cols].astype(f32) + r2[1 - k, :, cols].astype(f32)
+            res[rows(place(l, k, x, y), eighth), dest] = (factor * apart).astype(bf16)
+
         def body(j, _):
-            cols = rows(offset[l] + j * BLK, BLK)
             for k, own in turns:
-                here = rows(eighth * own, eighth)
-                apart = keep[k, here, cols] + r1[k, here, cols].astype(f32) + r2[1 - k, :, cols].astype(f32)
-                res[rows(place(l, k, x, y), eighth), rows(j * BLK, BLK)] = (factor * apart).astype(bf16)
-            return 0
-
-        lax.fori_loop(0, l + 1, body, 0)
+                add(k, own, rows(offset[l] + j * BLK, BLK), rows(j * BLK, BLK))
+            return 0
+
+        lax.fori_loop(0, l, body, 0)
+        for k, own in turns:
+            size = half if k == 0 else BLK
+            add(k, own, pl.ds(offset[l] + l * BLK, size), pl.ds(l * BLK, size))
 
     def gather(l, slot, k, px, py, to):
-        area = res.at[rows(place(l, k, px, py), eighth), pl.ds(0, (l + 1) * BLK)]
+        area = res.at[rows(place(l, k, px, py), eighth), pl.ds(0, reach(l, k))]
         return push(area, area, ag_send.at[slot, l], ag_recv.at[slot, l], to)
 
     def own_rows(l):
@@ -477,20 +489,21 @@
         gather(l, 5, 1, 1 - x, 1 - y, across).wait_recv()
 
     def multiply(l):
-        start, stop = l * BLK, (l + 1) * BLK
+        start, stop, mid = l * BLK, (l + 1) * BLK, l * BLK + half
+        res[start:mid, mid:stop] = res[mid:stop, start:mid].T
         out = jnp.dot(res[start:stop, 0:stop], nrm[0:stop], preferred_element_type=f32)
         if stop < length:
             out = out + lax.dot_general(
                 res[stop:length, start:stop], nrm[stop:length], (((0,), (0,)), ((), ())), preferred_element_type=f32
             )
-        gbuf[l % 2] = out
+        gbuf[l % 3] = out
 
         def body(i, _):
             local = rows(i * TILE, TILE)
             at = rows(start + i * TILE, TILE)
             inner = jnp.zeros((TILE, 128), f32)
             for lane in lanes:
-                inner = inner + hid[at, lane].astype(f32) * invc[at] * gbuf[l % 2, local, lane]
+                inner = inner + hid[at, lane].astype(f32) * invc[at] * gbuf[l % 3, local, lane]
             lane_sums[local] = inner
             return 0
 
@@ -506,7 +519,7 @@
             inverse, projection = invc[at], lane_sums[local]
             for lane in lanes:
                 normed = hid[at, lane].astype(f32) * inverse
-                hgrad[at, lane] = inverse * (gbuf[l % 2, local, lane] - normed * projection)
+                hgrad[at, lane] = inverse * (gbuf[l % 3, local, lane] - normed * projection)
             return 0
 
         lax.fori_loop(0, BLK // TILE, body, 0)
@@ -537,44 +550,52 @@
         lax.fori_loop(0, BLK // TILE, body, 0)
 
     order = ([blocks - 2, blocks - 1] + list(range(blocks - 3, -1, -1))) if blocks > 1 else [0]
-    conv(0)
-    pl.semaphore_wait(barrier, groups + rings - 2)
-    share(0, 0)
-    lag = 3
-    for t in range(1, blocks + lag + 2):
+    begin, hop = 2, 2
+    for t in range(blocks + begin + 2 * hop):
         if t < blocks:
             conv(t)
+            if t == 0:
+                pl.semaphore_wait(barrier, groups + rings - 2)
             share(0, t)
-        if t == lag:
+        l = t - begin
+        if l == 0:
             teach_copy.wait()
-        if 0 <= t - lag < blocks:
-            normalize(t - lag)
-            gram(t - lag)
-        if 0 <= t - lag - 1 < blocks:
-            combine(t - lag - 1)
-        if 0 <= t - lag - 2 < blocks:
-            l = t - lag - 2
+        if 0 <= l < blocks:
+            normalize(l)
+            gram(l)
+        l = l - hop
+        if 0 <= l < blocks:
+            combine(l)
+        l = l - hop
+        if 0 <= l < blocks:
             residue(l)
             if l in order[:2]:
                 for copy in own_rows(l):
                     copy.start()
+
+    def send_own(i):
+        if i < blocks:
+            for copy in own_rows(order[i]):
+                copy.start()
+
+    relay(order[0])
+    send_own(2)
     ready = []
     for i, l in enumerate(order):
-        relay(l)
-        if i + 2 < blocks:
-            for copy in own_rows(order[i + 2]):
-                copy.start()
         landed(l)
-        fresh = [] if i == 0 and blocks > 1 else ([blocks - 1, blocks - 2] if i == 1 else [l])
-        for at in fresh:
+        if i + 1 < blocks:
+            relay(order[i + 1])
+        send_own(i + 3)
+        for at in [] if i == 0 and blocks > 1 else ([blocks - 1, blocks - 2] if i == 1 else [l]):
             multiply(at)
             ready.append(at)
-            if len(ready) > 1:
+            if len(ready) > 2:
                 done = ready.pop(0)
                 finish(done)
                 back(done)
-    finish(ready[0])
-    back(ready[0])
+    for done in ready:
+        finish(done)
+        back(done)
 
     for b in range(2):
         for j in range(taps):
@@ -643,7 +664,7 @@
             pltpu.VMEM((2, BLK // 8, triangle), bf16),
             pltpu.VMEM((2, BLK // 8, triangle), bf16),
             pltpu.VMEM((length, length), bf16),
-            pltpu.VMEM((2, BLK, width), f32),
+            pltpu.VMEM((3, BLK, width), f32),
             pltpu.VMEM((length + PAD, width), f32),
             pltpu.VMEM((BLK, 128), f32),
             pltpu.VMEM((2, 4, blocks, 8, BLK), f32),

time: 131 us -> 113 us (0.86)
  Pallas kernels: 126 us -> 109 us
    pallas_call x1, Pallas kernels: 126 us -> 109 us  [quad_call(): pl.pallas_call(functools.partial(quad_kernel, rings, taps, norm_factor),...]
where the time goes in v2:
time: 113 us
  Pallas kernels  109 us (96%)
  local copies, waits for them, and re-layouts  3.86 us (3%)
    pallas_call x1, Pallas kernels, quad_call(): pl.pallas_call(functools.partial(quad_kernel, rings, taps, norm_factor),...  109 us
    unnamed x8, local copies, waits for them, and re-layouts  3.86 us

profile of v2, /device:TPU:0, one launch (start us, length us, event | category | flops | bytes accessed | tf_op | source)
XLA Modules:
  0.0 113.0 jit_solution(1240718594197798564)
XLA Ops:
  0.6 108.5 %shard_map.84 = (bf16[1,2048,512]{2,1,0:T(8,128)(2,1)S(1)}, bf16[1,2048,512]{2,1,0:T(8,128)(2,1)S(1)}, f32[7,512]{1,0:T(8,128)}, f32[7,512]{1,0:T(8,128)}) custom-call(bf16[1,2048,512]{2,1,0:T(8,128)(2,1)} %gate_in.1, bf16[1,2048,512]{2,1,0:T(8,128)(2,1)} %value_in.1, f32[7,512]{1,0:T(8,128)} %filter_gate.1, f32[7,512]{1,0:T(8,128)} %filter_value.1, ...), custom_call_target="tpu_custom_call" | custom-call | tf_op jit(solution)/shard_map/pallas_call | solution.py:642
  109.2 1.3 %copy.13 = bf16[1,2048,512]{2,1,0:T(8,128)(2,1)} copy(bf16[1,2048,512]{2,1,0:T(8,128)(2,1)S(1)} %get-tuple-element.4) | data formatting | bytes 4194304
  110.5 0.0 copy-start.1
  110.5 0.0 copy-start
  110.5 1.3 %copy.14 = bf16[1,2048,512]{2,1,0:T(8,128)(2,1)} copy(bf16[1,2048,512]{2,1,0:T(8,128)(2,1)S(1)} %get-tuple-element.5) | data formatting | bytes 4194304
  111.8 0.0 copy-done.1
  111.8 0.6 copy.15
  112.4 0.0 copy-done
  112.4 0.6 copy.16
Async XLA Ops:
  110.5 1.3 %copy-start.1 = (f32[7,512]{1,0:T(8,128)S(1)}, f32[7,512]{1,0:T(8,128)}, u32[]{:S(2)}) copy-start(f32[7,512]{1,0:T(8,128)} %get-tuple-element.14) | copy-start | bytes 43012
  110.5 1.9 %copy-start = (f32[7,512]{1,0:T(8,128)S(1)}, f32[7,512]{1,0:T(8,128)}, u32[]{:S(2)}) copy-start(f32[7,512]{1,0:T(8,128)} %get-tuple-element.15) | copy-start | bytes 43012

commit v3 on v2

--- a/solution.py
+++ b/solution.py
@@ -12,6 +12,9 @@
 PAD = 16
 TILE = 64
 BLK = 256
+EARLY = 0
+LAG = 2
+SPLIT = True
 MESH = pl.DeviceIdType.MESH
 
 
@@ -488,22 +491,37 @@
         gather(l, 4, 0, 1 - x, 1 - y, along).wait_recv()
         gather(l, 5, 1, 1 - x, 1 - y, across).wait_recv()
 
-    def multiply(l):
+    def lower(l):
         start, stop, mid = l * BLK, (l + 1) * BLK, l * BLK + half
         res[start:mid, mid:stop] = res[mid:stop, start:mid].T
-        out = jnp.dot(res[start:stop, 0:stop], nrm[0:stop], preferred_element_type=f32)
-        if stop < length:
-            out = out + lax.dot_general(
-                res[stop:length, start:stop], nrm[stop:length], (((0,), (0,)), ((), ())), preferred_element_type=f32
-            )
-        gbuf[l % 3] = out
-
+        return jnp.dot(res[start:stop, 0:stop], nrm[0:stop], preferred_element_type=f32)
+
+    def upper(l, begin, end):
+        if begin == end:
+            return 0.0
+        return lax.dot_general(
+            res[begin * BLK : end * BLK, l * BLK : (l + 1) * BLK], nrm[begin * BLK : end * BLK],
+            (((0,), (0,)), ((), ())), preferred_element_type=f32,
+        )
+
+    def multiply(l):
+        gbuf[l] = lower(l) + upper(l, l + 1, blocks)
+        project(l)
+
+    def prepare(l, late):
+        gbuf[l] = lower(l) + upper(l, l + 1, late) + upper(l, late + 1, blocks)
+
+    def complete(l, late):
+        gbuf[l] += upper(l, late, late + 1)
+        project(l)
+
+    def project(l):
         def body(i, _):
             local = rows(i * TILE, TILE)
-            at = rows(start + i * TILE, TILE)
+            at = rows(l * BLK + i * TILE, TILE)
             inner = jnp.zeros((TILE, 128), f32)
             for lane in lanes:
-                inner = inner + hid[at, lane].astype(f32) * invc[at] * gbuf[l % 3, local, lane]
+                inner = inner + hid[at, lane].astype(f32) * invc[at] * gbuf[l, local, lane]
             lane_sums[local] = inner
             return 0
 
@@ -519,12 +537,12 @@
             inverse, projection = invc[at], lane_sums[local]
             for lane in lanes:
                 normed = hid[at, lane].astype(f32) * inverse
-                hgrad[at, lane] = inverse * (gbuf[l % 3, local, lane] - normed * projection)
+                hgrad[at, lane] = inverse * (gbuf[l, local, lane] - normed * projection)
             return 0
 
         lax.fori_loop(0, BLK // TILE, body, 0)
 
-    def back(l):
+    def back(l, tapped=True, stored=True):
         def body(i, _):
             base = pl.multiple_of(l * BLK + i * TILE, TILE)
             for lane in lanes:
@@ -537,19 +555,24 @@
                     out = None
                     for j in range(taps):
                         shifted = (window if j == 0 else pltpu.roll(window, TILE + PAD - j, 0))[:TILE]
-                        term = weights[j : j + 1, lane] * shifted
-                        out = term if out is None else out + term
-                        product = shifted * signal
-                        folded = product[0:8]
-                        for r in range(8, TILE, 8):
-                            folded = folded + product[r : r + 8]
-                        sums[b, j, :, lane] += folded
-                    store[0, pl.ds(base, TILE), lane] = out.astype(bf16)
+                        if stored:
+                            term = weights[j : j + 1, lane] * shifted
+                            out = term if out is None else out + term
+                        if tapped:
+                            product = shifted * signal
+                            folded = product[0:8]
+                            for r in range(8, TILE, 8):
+                                folded = folded + product[r : r + 8]
+                            sums[b, j, :, lane] += folded
+                    if stored:
+                        store[0, pl.ds(base, TILE), lane] = out.astype(bf16)
             return 0
 
         lax.fori_loop(0, BLK // TILE, body, 0)
 
-    order = ([blocks - 2, blocks - 1] + list(range(blocks - 3, -1, -1))) if blocks > 1 else [0]
+    early = max(0, min(EARLY, blocks - 4))
+    order = list(range(blocks - 1, early - 1, -1))
+    order[:2] = order[1::-1]
     begin, hop = 2, 2
     for t in range(blocks + begin + 2 * hop):
         if t < blocks:
@@ -569,12 +592,15 @@
         l = l - hop
         if 0 <= l < blocks:
             residue(l)
-            if l in order[:2]:
+            if l < early or l in order[:2]:
                 for copy in own_rows(l):
                     copy.start()
+        l = l - hop
+        if 0 <= l < early:
+            relay(l)
 
     def send_own(i):
-        if i < blocks:
+        if i < len(order):
             for copy in own_rows(order[i]):
                 copy.start()
 
@@ -582,20 +608,34 @@
     send_own(2)
     ready = []
     for i, l in enumerate(order):
+        final = i == len(order) - 1
+        if final:
+            for at in range(early):
+                landed(at)
+                prepare(at, l)
+        if i:
+            send_own(i + 2)
+        if not final:
+            relay(order[i + 1])
         landed(l)
-        if i + 1 < blocks:
-            relay(order[i + 1])
-        send_own(i + 3)
         for at in [] if i == 0 and blocks > 1 else ([blocks - 1, blocks - 2] if i == 1 else [l]):
             multiply(at)
             ready.append(at)
-            if len(ready) > 2:
+            if len(ready) > LAG and not final:
                 done = ready.pop(0)
                 finish(done)
                 back(done)
+    for at in reversed(range(early)):
+        complete(at, order[-1])
+    while len(ready) > 1:
+        done = ready.pop(0)
+        finish(done)
+        back(done)
+    ready = ready + list(reversed(range(early)))
     for done in ready:
         finish(done)
-        back(done)
+    for done in ready:
+        back(done, stored=not SPLIT)
 
     for b in range(2):
         for j in range(taps):
@@ -611,6 +651,8 @@
     ]
     for copy in tap_copies:
         copy.start()
+    for done in ready if SPLIT else []:
+        back(done, tapped=False)
     for l in range(blocks):
         for copy in (*stage_one(l), *stage_two(l), *own_rows(l), *relays(l)):
             copy.wait_send()
@@ -639,13 +681,13 @@
     any_space = pl.BlockSpec(memory_space=pl.ANY)
     vmem = pl.BlockSpec(memory_space=pltpu.VMEM)
     dma = pltpu.SemaphoreType.DMA
-    return pl.pallas_call(
+    made = pl.pallas_call(
         functools.partial(quad_kernel, rings, taps, norm_factor),
         out_shape=(
             pltpu.VMEM(gate_raw.shape, bf16),
             pltpu.VMEM(gate_raw.shape, bf16),
-            jax.ShapeDtypeStruct((taps, width), f32),
-            jax.ShapeDtypeStruct((taps, width), f32),
+            pltpu.VMEM((taps, width), f32),
+            pltpu.VMEM((taps, width), f32),
         ),
         in_specs=[any_space, any_space, vmem, vmem, any_space],
         out_specs=(vmem, vmem, vmem, vmem),
@@ -664,7 +706,7 @@
             pltpu.VMEM((2, BLK // 8, triangle), bf16),
             pltpu.VMEM((2, BLK // 8, triangle), bf16),
             pltpu.VMEM((length, length), bf16),
-            pltpu.VMEM((3, BLK, width), f32),
+            pltpu.VMEM((blocks, BLK, width), f32),
             pltpu.VMEM((length + PAD, width), f32),
             pltpu.VMEM((BLK, 128), f32),
             pltpu.VMEM((2, 4, blocks, 8, BLK), f32),
@@ -688,6 +730,23 @@
             collective_id=0, has_side_effects=True, vmem_limit_bytes=58 * 1024 * 1024
         ),
     )(gate_raw, value_raw, filter_gate, filter_value, teacher)
+    return pl.pallas_call(
+        store_kernel,
+        out_shape=tuple(jax.ShapeDtypeStruct(array.shape, array.dtype) for array in made),
+        in_specs=[vmem] * 4,
+        out_specs=(any_space,) * 4,
+        scratch_shapes=[dma((4,))],
+        compiler_params=pltpu.CompilerParams(vmem_limit_bytes=1024 * 1024),
+    )(*made)
+
+
+def store_kernel(*refs):
+    sems = refs[8]
+    copies = [pltpu.make_async_copy(refs[k], refs[4 + k], sems.at[k]) for k in range(4)]
+    for copy in copies:
+        copy.start()
+    for copy in copies:
+        copy.wait()
 
 
 def stripe_call(gate_raw, value_raw, filter_gate, filter_value, teacher):

time: 113 us -> 110 us (0.973)
  local copies, waits for them, and re-layouts: 3.86 us -> 0 us
    unnamed x8 -> x0, local copies, waits for them, and re-layouts: 3.86 us -> none
    pallas_call x0 -> x1, Pallas kernels: none -> 2.05 us  [quad_call(): pl.pallas_call(store_kernel, out_shape=tuple((jax.ShapeDtypeStruct(array....]
    pallas_call x1, Pallas kernels: 109 us -> 107 us  [quad_call(): pl.pallas_call(functools.partial(quad_kernel, rings, taps, norm_factor),...]
where the time goes in v3:
time: 110 us
  Pallas kernels  109 us (99%)
    pallas_call x1, Pallas kernels, quad_call(): pl.pallas_call(functools.partial(quad_kernel, rings, taps, norm_factor),...  107 us

profile of v3, /device:TPU:0, one launch (start us, length us, event | category | flops | bytes accessed | tf_op | source)
XLA Modules:
  0.0 109.6 jit_solution(9307811856439711000)
XLA Ops:
  0.6 106.9 %shard_map.84 = (bf16[1,2048,512]{2,1,0:T(8,128)(2,1)S(1)}, bf16[1,2048,512]{2,1,0:T(8,128)(2,1)S(1)}, f32[7,512]{1,0:T(8,128)S(1)}, f32[7,512]{1,0:T(8,128)S(1)}) custom-call(bf16[1,2048,512]{2,1,0:T(8,128)(2,1)} %gate_in.1, bf16[1,2048,512]{2,1,0:T(8,128)(2,1)} %value_in.1, f32[7,512]{1,0:T(8,128)} %filter_gate.1, f32[7,512]{1,0:T(8,128)} %filter_value.1, ...), custom_call_target="tpu_custom_call" | custom-call | tf_op jit(solution)/shard_map/pallas_call | solution.py:684
  107.5 2.1 %shard_map.85 = (bf16[1,2048,512]{2,1,0:T(8,128)(2,1)}, bf16[1,2048,512]{2,1,0:T(8,128)(2,1)}, f32[7,512]{1,0:T(8,128)}, f32[7,512]{1,0:T(8,128)}) custom-call(bf16[1,2048,512]{2,1,0:T(8,128)(2,1)S(1)} %get-tuple-element.8.refs_0_, bf16[1,2048,512]{2,1,0:T(8,128)(2,1)S(1)} %get-tuple-element.9.refs_1_, f32[7,512]{1,0:T(8,128)S(1)} %get-tuple-element.10.refs_2_, ...), custom_call_target="tpu_custom_call" | custom-call | tf_op jit(solution)/shard_map/pallas_call | solution.py:733

commit v4 on v3

--- a/solution.py
+++ b/solution.py
@@ -573,7 +573,7 @@
     early = max(0, min(EARLY, blocks - 4))
     order = list(range(blocks - 1, early - 1, -1))
     order[:2] = order[1::-1]
-    begin, hop = 2, 2
+    begin, hop = 3, 3
     for t in range(blocks + begin + 2 * hop):
         if t < blocks:
             conv(t)

time: 110 us -> 110 us (level)
  no operation moved by 1% of the time
where the time goes in v4:
time: 110 us; the launch traced here: 109 us
  Pallas kernels  109 us (99%)
    pallas_call x1, Pallas kernels, quad_call(): pl.pallas_call(functools.partial(quad_kernel, rings, taps, norm_factor),...  107 us

profile of v4, /device:TPU:0, one launch (start us, length us, event | category | flops | bytes accessed | tf_op | source)
XLA Modules:
  0.0 109.2 jit_solution(7937455937565897447)
XLA Ops:
  0.6 106.5 %shard_map.84 = (bf16[1,2048,512]{2,1,0:T(8,128)(2,1)S(1)}, bf16[1,2048,512]{2,1,0:T(8,128)(2,1)S(1)}, f32[7,512]{1,0:T(8,128)S(1)}, f32[7,512]{1,0:T(8,128)S(1)}) custom-call(bf16[1,2048,512]{2,1,0:T(8,128)(2,1)} %gate_in.1, bf16[1,2048,512]{2,1,0:T(8,128)(2,1)} %value_in.1, f32[7,512]{1,0:T(8,128)} %filter_gate.1, f32[7,512]{1,0:T(8,128)} %filter_value.1, ...), custom_call_target="tpu_custom_call" | custom-call | tf_op jit(solution)/shard_map/pallas_call | solution.py:684
  107.2 2.1 %shard_map.85 = (bf16[1,2048,512]{2,1,0:T(8,128)(2,1)}, bf16[1,2048,512]{2,1,0:T(8,128)(2,1)}, f32[7,512]{1,0:T(8,128)}, f32[7,512]{1,0:T(8,128)}) custom-call(bf16[1,2048,512]{2,1,0:T(8,128)(2,1)S(1)} %get-tuple-element.8.refs_0_, bf16[1,2048,512]{2,1,0:T(8,128)(2,1)S(1)} %get-tuple-element.9.refs_1_, f32[7,512]{1,0:T(8,128)S(1)} %get-tuple-element.10.refs_2_, ...), custom_call_target="tpu_custom_call" | custom-call | tf_op jit(solution)/shard_map/pallas_call | solution.py:733

commit v5 on v4

--- a/solution.py
+++ b/solution.py
@@ -627,14 +627,13 @@
                 back(done)
     for at in reversed(range(early)):
         complete(at, order[-1])
-    while len(ready) > 1:
+    while len(ready) > 2:
         done = ready.pop(0)
         finish(done)
         back(done)
     ready = ready + list(reversed(range(early)))
     for done in ready:
         finish(done)
-    for done in ready:
         back(done, stored=not SPLIT)
 
     for b in range(2):

time: 110 us -> 109 us (level)
  no operation moved by 1% of the time
where the time goes in v5:
time: 109 us
  Pallas kernels  108 us (99%)
    pallas_call x1, Pallas kernels, quad_call(): pl.pallas_call(functools.partial(quad_kernel, rings, taps, norm_factor),...  106 us

profile of v5, /device:TPU:0, one launch (start us, length us, event | category | flops | bytes accessed | tf_op | source)
XLA Modules:
  0.0 109.0 jit_solution(13925593964048178960)
XLA Ops:
  0.6 106.3 %shard_map.84 = (bf16[1,2048,512]{2,1,0:T(8,128)(2,1)S(1)}, bf16[1,2048,512]{2,1,0:T(8,128)(2,1)S(1)}, f32[7,512]{1,0:T(8,128)S(1)}, f32[7,512]{1,0:T(8,128)S(1)}) custom-call(bf16[1,2048,512]{2,1,0:T(8,128)(2,1)} %gate_in.1, bf16[1,2048,512]{2,1,0:T(8,128)(2,1)} %value_in.1, f32[7,512]{1,0:T(8,128)} %filter_gate.1, f32[7,512]{1,0:T(8,128)} %filter_value.1, ...), custom_call_target="tpu_custom_call" | custom-call | tf_op jit(solution)/shard_map/pallas_call | solution.py:683
  107.0 2.1 %shard_map.85 = (bf16[1,2048,512]{2,1,0:T(8,128)(2,1)}, bf16[1,2048,512]{2,1,0:T(8,128)(2,1)}, f32[7,512]{1,0:T(8,128)}, f32[7,512]{1,0:T(8,128)}) custom-call(bf16[1,2048,512]{2,1,0:T(8,128)(2,1)S(1)} %get-tuple-element.8.refs_0_, bf16[1,2048,512]{2,1,0:T(8,128)(2,1)S(1)} %get-tuple-element.9.refs_1_, f32[7,512]{1,0:T(8,128)S(1)} %get-tuple-element.10.refs_2_, ...), custom_call_target="tpu_custom_call" | custom-call | tf_op jit(solution)/shard_map/pallas_call | solution.py:732
